TPU v7x, 32 devices: a whole 2x2x4 slice. The times are simulated.
32 devices in a mesh: dp: 4 (over y, core), fsdp: 8 (over z, x).
Axes of the slice: x: 2, y: 2, z: 4, core: 2. Of those that a mesh axis runs over, the one named last changes fastest.
Arguments:
- hidden_in: bfloat16 [2, 32, 1024, 576], P(None, ('dp', 'fsdp')), may hold values from -0.59765625 to 0.59765625
- seg_ids: int32 [2, 32, 1024], P(None, ('dp', 'fsdp')), may hold values from 0 to 7, never falling along the last dimension, each value on 1 to 512 neighbouring positions
- out_grad: bfloat16 [2, 32, 1024, 576], P(None, ('dp', 'fsdp')), may hold values from -6 to 6
- gains: float32 [2, 576], P(None, 'fsdp'), may hold values from 0.5 to 1.5
- matrices: float32 [576, 6144], P('fsdp'), may hold values from -8 to 8
- gain_momentum: float32 [2, 576], P(None, 'fsdp'), may hold values from -0.3 to 0.3
- mat_momentum: float32 [576, 6144], P('fsdp'), may hold values from -0.12 to 0.12
Outputs:
- out_hidden: bfloat16 [2, 32, 1024, 576], P(None, ('dp', 'fsdp'))
- in_grad: float32 [2, 32, 1024, 576], P(None, ('dp', 'fsdp'))
- matrix_grad: float32 [576, 6144], P('fsdp')
- gain_grad: float32 [2, 576], P(None, 'fsdp')
- new_mat_momentum: float32 [576, 6144], P('fsdp')
- new_gain_momentum: float32 [2, 576], P(None, 'fsdp')
- new_matrices: float32 [576, 6144], P('fsdp')
- new_gains: float32 [2, 576], P(None, 'fsdp')
Inputs may be any that keep to these rules, and one draw needn't show every extreme that they name: `seg_ids`: within a sequence segment numbers never fall; a document holds at most 512 tokens.
All inputs are finite; a program needn't handle non-finite values.
Results may differ from a plain program's by a relative error of at most 0.01.
The roundings to bfloat16 on the way count: a program that leaves them out, or rounds other values in their place, can miss the bound.
Values may be sent and summed in bfloat16 or wider, within the bound.
A program may use at most 384 MiB of HBM per device.

v0:
```python
import math

import jax
import jax.numpy as jnp
from jax import lax
from jax.sharding import PartitionSpec as P

D = 576
HEADS = 9
KVH = 3
HD = 64
FF = 1536
QB = 512
NS_STEPS = 5


HIGH = lax.Precision.HIGHEST
EPS_NORM = 1e-05
ROPE_BASE = 100000.0
MOMENT = 0.95
LEARN = 0.05
GAIN_LEARN = 0.1
COEF_A = 3.4445
COEF_B = -4.775
COEF_C = 2.0315
DIMS_ROWS = (((0,), (0,)), ((), ()))
DIMS_COLS = (((1,), (1,)), ((), ()))


def rope_tables(segment):
    seq_len = segment.shape[0]
    token_index = jnp.arange(seq_len, dtype=jnp.int32)
    first_mark = jnp.concatenate([jnp.ones((1,), dtype=bool), segment[1:] != segment[:-1]])
    start_index = lax.cummax(jnp.where(first_mark, token_index, 0), axis=0)
    offset = (token_index - start_index).astype(jnp.float32)
    inverse = 1.0 / ROPE_BASE ** (jnp.arange(0, HD, 2, dtype=jnp.float32) / HD)
    angle = offset[:, None] * inverse[None, :]
    return (jnp.cos(angle)[:, None, :], jnp.sin(angle)[:, None, :])


def rotate(values, cosine, sine):
    half_dim = values.shape[-1] // 2
    first_half = values[..., :half_dim]
    second_half = values[..., half_dim:]
    return jnp.concatenate(
        [first_half * cosine - second_half * sine, second_half * cosine + first_half * sine],
        axis=-1,
    )


def rotate_back(grads, cosine, sine):
    half_dim = grads.shape[-1] // 2
    first_half = grads[..., :half_dim]
    second_half = grads[..., half_dim:]
    return jnp.concatenate(
        [first_half * cosine + second_half * sine, second_half * cosine - first_half * sine],
        axis=-1,
    )


def attention_scores(query_blk, key_rows, segment, start_row, stop_row):
    scores = (
        jnp.einsum("qkgd,tkd->kgqt", query_blk, key_rows, preferred_element_type=jnp.float32)
        * 0.125
    )
    query_pos = start_row + jnp.arange(stop_row - start_row, dtype=jnp.int32)
    key_pos = jnp.arange(stop_row, dtype=jnp.int32)
    allowed = (key_pos[None, :] <= query_pos[:, None]) & (
        segment[:stop_row][None, :] == segment[start_row:stop_row][:, None]
    )
    return (scores, allowed)


def forward_pass(inputs, segment, weights, gain_pair):
    seq_len = inputs.shape[0]
    kv_cols = KVH * HD
    group_size = HEADS // KVH
    block_rows = min(QB, seq_len)
    cosine, sine = rope_tables(segment)
    r_one = lax.rsqrt(jnp.mean(inputs * inputs, axis=-1, keepdims=True) + EPS_NORM)
    u_one = inputs * r_one
    a_low = (u_one * gain_pair[0]).astype(jnp.bfloat16)
    projected = jnp.dot(a_low, weights[:, : D + 2 * kv_cols], preferred_element_type=jnp.float32)
    query_rot = (
        rotate(projected[:, :D].reshape(seq_len, HEADS, HD), cosine, sine)
        .astype(jnp.bfloat16)
        .reshape(seq_len, KVH, group_size, HD)
    )
    key_rot = rotate(projected[:, D : D + kv_cols].reshape(seq_len, KVH, HD), cosine, sine).astype(
        jnp.bfloat16
    )
    value_low = projected[:, D + kv_cols :].astype(jnp.bfloat16).reshape(seq_len, KVH, HD)
    head_out = []
    log_sums = []
    for block_id in range(seq_len // block_rows):
        start_row = block_id * block_rows
        stop_row = start_row + block_rows
        scores, allowed = attention_scores(
            query_rot[start_row:stop_row], key_rot[:stop_row], segment, start_row, stop_row
        )
        scores = jnp.where(allowed, scores, -1e30)
        row_max = jnp.max(scores, axis=-1, keepdims=True)
        exponent = jnp.exp(scores - row_max)
        row_total = jnp.sum(exponent, axis=-1, keepdims=True)
        probs_low = (exponent / row_total).astype(jnp.bfloat16)
        head_out.append(
            jnp.einsum(
                "kgqt,tkd->qkgd",
                probs_low,
                value_low[:stop_row],
                preferred_element_type=jnp.float32,
            ).reshape(block_rows, D)
        )
        log_sums.append(row_max + jnp.log(row_total))
    mixed_low = jnp.concatenate(head_out, axis=0).astype(jnp.bfloat16)
    middle = inputs + jnp.dot(
        mixed_low, weights[:, D + 2 * kv_cols : FF], preferred_element_type=jnp.float32
    )
    r_two = lax.rsqrt(jnp.mean(middle * middle, axis=-1, keepdims=True) + EPS_NORM)
    u_two = middle * r_two
    b_low = (u_two * gain_pair[1]).astype(jnp.bfloat16)
    gate_up = jnp.dot(b_low, weights[:, FF : 3 * FF], preferred_element_type=jnp.float32)
    gate_pre = gate_up[:, :FF]
    up_pre = gate_up[:, FF:]
    inner_low = (jax.nn.silu(gate_pre) * up_pre).astype(jnp.bfloat16)
    result = middle + lax.dot_general(
        inner_low, weights[:, 3 * FF :], DIMS_COLS, preferred_element_type=jnp.float32
    )
    saved = (
        segment,
        cosine,
        sine,
        r_one,
        u_one,
        a_low,
        query_rot,
        key_rot,
        value_low,
        log_sums,
        mixed_low,
        r_two,
        u_two,
        b_low,
        gate_pre,
        up_pre,
        inner_low,
    )
    return (saved, result.astype(jnp.bfloat16))


def backward_pass(saved, cotangent, weights, gain_pair):
    (
        segment,
        cosine,
        sine,
        r_one,
        u_one,
        a_low,
        query_rot,
        key_rot,
        value_low,
        log_sums,
        mixed_low,
        r_two,
        u_two,
        b_low,
        gate_pre,
        up_pre,
        inner_low,
    ) = saved
    seq_len = cotangent.shape[0]
    kv_cols = KVH * HD
    group_size = HEADS // KVH
    block_rows = min(QB, seq_len)
    d_branch = cotangent.astype(jnp.bfloat16)
    grad_down = lax.dot_general(d_branch, inner_low, DIMS_ROWS, preferred_element_type=jnp.float32)
    d_inner = jnp.dot(d_branch, weights[:, 3 * FF :], preferred_element_type=jnp.float32)
    sigma = jax.nn.sigmoid(gate_pre)
    silu_val = gate_pre * sigma
    d_gate = (d_inner * up_pre * sigma * (1.0 + gate_pre * (1.0 - sigma))).astype(jnp.bfloat16)
    d_up = (d_inner * silu_val).astype(jnp.bfloat16)
    d_gate_up = jnp.concatenate([d_gate, d_up], axis=1)
    grad_gate_up = lax.dot_general(b_low, d_gate_up, DIMS_ROWS, preferred_element_type=jnp.float32)
    d_norm_two = lax.dot_general(
        d_gate_up, weights[:, FF : 3 * FF], DIMS_COLS, preferred_element_type=jnp.float32
    )
    grad_gain_two = jnp.sum(d_norm_two * u_two, axis=0)
    d_unit_two = d_norm_two * gain_pair[1]
    d_middle = (
        r_two * (d_unit_two - u_two * jnp.mean(d_unit_two * u_two, axis=-1, keepdims=True))
        + cotangent
    )
    d_attn = d_middle.astype(jnp.bfloat16)
    grad_out = lax.dot_general(mixed_low, d_attn, DIMS_ROWS, preferred_element_type=jnp.float32)
    d_mixed = lax.dot_general(
        d_attn, weights[:, D + 2 * kv_cols : FF], DIMS_COLS, preferred_element_type=jnp.float32
    ).astype(jnp.bfloat16)
    query_grads = []
    d_key = jnp.zeros((seq_len, KVH, HD), jnp.float32)
    d_value = jnp.zeros((seq_len, KVH, HD), jnp.float32)
    for block_id in range(seq_len // block_rows):
        start_row = block_id * block_rows
        stop_row = start_row + block_rows
        query_blk = query_rot[start_row:stop_row]
        scores, allowed = attention_scores(
            query_blk, key_rot[:stop_row], segment, start_row, stop_row
        )
        probs = jnp.where(allowed, jnp.exp(scores - log_sums[block_id]), 0.0)
        probs_low = probs.astype(jnp.bfloat16)
        d_out_blk = d_mixed[start_row:stop_row].reshape(block_rows, KVH, group_size, HD)
        d_probs = jnp.einsum(
            "qkgd,tkd->kgqt", d_out_blk, value_low[:stop_row], preferred_element_type=jnp.float32
        )
        d_scores = (probs * (d_probs - jnp.sum(d_probs * probs, axis=-1, keepdims=True))).astype(
            jnp.bfloat16
        )
        query_grads.append(
            jnp.einsum(
                "kgqt,tkd->qkgd", d_scores, key_rot[:stop_row], preferred_element_type=jnp.float32
            )
            * 0.125
        )
        d_key = d_key.at[:stop_row].add(
            jnp.einsum("kgqt,qkgd->tkd", d_scores, query_blk, preferred_element_type=jnp.float32)
            * 0.125
        )
        d_value = d_value.at[:stop_row].add(
            jnp.einsum("kgqt,qkgd->tkd", probs_low, d_out_blk, preferred_element_type=jnp.float32)
        )
    d_query_rot = jnp.concatenate(query_grads, axis=0).reshape(seq_len, HEADS, HD)
    d_query = rotate_back(d_query_rot, cosine, sine).reshape(seq_len, D)
    d_key_pre = rotate_back(d_key, cosine, sine).reshape(seq_len, kv_cols)
    d_project = jnp.concatenate(
        [d_query, d_key_pre, d_value.reshape(seq_len, kv_cols)], axis=1
    ).astype(jnp.bfloat16)
    grad_project = lax.dot_general(a_low, d_project, DIMS_ROWS, preferred_element_type=jnp.float32)
    d_norm_one = lax.dot_general(
        d_project, weights[:, : D + 2 * kv_cols], DIMS_COLS, preferred_element_type=jnp.float32
    )
    grad_gain_one = jnp.sum(d_norm_one * u_one, axis=0)
    d_unit_one = d_norm_one * gain_pair[0]
    d_input = (
        r_one * (d_unit_one - u_one * jnp.mean(d_unit_one * u_one, axis=-1, keepdims=True))
        + d_middle
    )
    grad_weights = jnp.concatenate([grad_project, grad_out, grad_gate_up, grad_down], axis=1)
    grad_gains = jnp.stack([grad_gain_one, grad_gain_two], axis=0)
    return (d_input, grad_weights, grad_gains)


def orthogonal(matrix):
    tall = matrix.shape[0] > matrix.shape[1]
    work = matrix.T if tall else matrix
    work = work / (jnp.sqrt(jnp.sum(work * work)) + 1e-07)
    for sweep_id in range(NS_STEPS):
        gram = jnp.dot(work, work.T, precision=HIGH)
        poly = COEF_B * gram + COEF_C * jnp.dot(gram, gram, precision=HIGH)
        work = COEF_A * work + jnp.dot(poly, work, precision=HIGH)
    if tall:
        work = work.T
    return work * (0.2 * math.sqrt(max(matrix.shape)))


def attention_block(block):
    kv_cols = KVH * HD
    bounds = [0, D, D + kv_cols, D + 2 * kv_cols, FF]
    pieces = [
        orthogonal(block[:, bounds[block_id] : bounds[block_id + 1]]) for block_id in range(4)
    ]
    return jnp.concatenate(pieces, axis=1)


def feed_block(block):
    return orthogonal(block)


def on_device(hidden_in, seg_ids, out_grad, gains, matrices, gain_momentum, mat_momentum):
    shard_rows = matrices.shape[0]
    total_cols = matrices.shape[1]
    full_rows = shard_rows * lax.axis_size("fsdp")
    total_tokens = (
        hidden_in.shape[0]
        * hidden_in.shape[1]
        * hidden_in.shape[2]
        * lax.axis_size("dp")
        * lax.axis_size("fsdp")
    )
    grad_scale = float(total_tokens) ** (-0.5)
    shard_low = matrices.astype(jnp.bfloat16)
    gain_low = gains.T.astype(jnp.bfloat16)

    def micro_step(running, element):
        inputs, segment, cotangent = element
        weights, gain_rows = (
            lax.all_gather(shard_low, "fsdp", axis=0, tiled=True),
            lax.all_gather(gain_low, "fsdp", axis=0, tiled=True),
        )
        gain_pair = gain_rows.astype(jnp.float32).T
        saved, result = forward_pass(inputs.astype(jnp.float32), segment, weights, gain_pair)
        weights_back, gain_back = (
            lax.all_gather(shard_low, "fsdp", axis=0, tiled=True),
            lax.all_gather(gain_low, "fsdp", axis=0, tiled=True),
        )
        gain_pair_back = gain_back.astype(jnp.float32).T
        d_input, grad_weights, grad_gains = backward_pass(
            saved, cotangent.astype(jnp.float32), weights_back, gain_pair_back
        )
        running = (running[0] + grad_weights, running[1] + grad_gains.T)
        return (running, (result, d_input))

    start_acc = (
        jnp.zeros((full_rows, total_cols), jnp.float32),
        jnp.zeros((full_rows, 2), jnp.float32),
    )
    totals, outputs = lax.scan(
        micro_step, start_acc, (hidden_in[:, 0], seg_ids[:, 0], out_grad[:, 0])
    )
    shard_weights, shard_gains = (
        lax.psum_scatter(totals[0], "fsdp", scatter_dimension=0, tiled=True),
        lax.psum_scatter(totals[1], "fsdp", scatter_dimension=0, tiled=True),
    )
    summed_weights, summed_gains = lax.psum((shard_weights, shard_gains), "dp")
    matrix_grad = summed_weights * grad_scale
    gain_grad = (summed_gains * grad_scale).T
    new_mat_momentum = MOMENT * mat_momentum + matrix_grad
    new_gain_momentum = MOMENT * gain_momentum + gain_grad
    look = matrix_grad + MOMENT * new_mat_momentum
    owner_group = lax.axis_index("dp")
    block_cols = total_cols // 4
    own_block = lax.dynamic_slice_in_dim(look, owner_group * block_cols, block_cols, 1)
    whole_block, whole_gain_mom = (
        lax.all_gather(own_block, "fsdp", axis=0, tiled=True),
        lax.all_gather(new_gain_momentum.T, "fsdp", axis=0, tiled=True),
    )
    orthogonal_block = lax.switch(
        owner_group, [attention_block, feed_block, feed_block, feed_block], whole_block
    )
    own_rows = lax.dynamic_slice_in_dim(
        orthogonal_block, lax.axis_index("fsdp") * shard_rows, shard_rows, 0
    )
    update_rows = lax.all_gather(own_rows, "dp", axis=1, tiled=True)
    new_matrices = matrices - LEARN * update_rows
    spread = lax.rsqrt(jnp.mean(whole_gain_mom * whole_gain_mom, axis=0, keepdims=True) + 1e-06)
    new_gains = gains - GAIN_LEARN * new_gain_momentum * spread.T
    out_hidden = outputs[0][:, None]
    in_grad = outputs[1][:, None]
    return (
        out_hidden,
        in_grad,
        matrix_grad,
        gain_grad,
        new_mat_momentum,
        new_gain_momentum,
        new_matrices,
        new_gains,
    )


def solution(mesh):
    in_specs = (
        P(None, ("dp", "fsdp"), None, None),
        P(None, ("dp", "fsdp"), None),
        P(None, ("dp", "fsdp"), None, None),
        P(None, "fsdp"),
        P("fsdp", None),
        P(None, "fsdp"),
        P("fsdp", None),
    )
    out_specs = (
        P(None, ("dp", "fsdp"), None, None),
        P(None, ("dp", "fsdp"), None, None),
        P("fsdp", None),
        P(None, "fsdp"),
        P("fsdp", None),
        P(None, "fsdp"),
        P("fsdp", None),
        P(None, "fsdp"),
    )
    return jax.shard_map(
        on_device, mesh=mesh, in_specs=in_specs, out_specs=out_specs, check_vma=False
    )
```

profile of v0, /device:TPU:7, one launch (start us, length us, event | category | flops | bytes accessed | tf_op | source)
XLA Modules:
  0.0 1255.4 jit_solution(15243894904164791844)
XLA Ops:
  11.0 645.1 %while.26 = (s32[]{:T(128)}, f32[576,6144]{1,0:T(8,128)}, f32[576,2]{0,1:T(2,128)}, bf16[2,1024,576]{1,2,0:T(8,128)(2,1)}, f32[2,1024,576]{1,2,0:T(8,128)}, /*in...) while((s32[]{:T(128)}, f32[576,6144]{1,0:T(8,128)}, ...), condition=%wide.region_15.16_spmd.clone, body=%wide.region_0.15_spmd.clone.sunk | while | flops 27494117376 | bytes 824622656 | solution.py:315
  12.7 13.4 %all-gather.4 = bf16[8,72,2]{1,2,0:T(2,128)(2,1)S(1)} all-gather(bf16[1,72,2]{1,2,0:T(2,128)(2,1)S(1)} %bitcast.639), channel_id=1, replica_groups=mesh['dp'=4,'fsdp'=8] {'fsdp'}, dimensions={0}, use_global_device_ids=true | all-gather | bytes 2592 | tf_op jit(solution)/shard_map/while/body/eval_jaxpr/all_gather | solution.py:296
  29.4 92.9 %all-gather.13.cloned.1.call-done = bf16[576,6144]{1,0:T(8,128)(2,1)} async-done(((bf16[72,6144]{1,0:T(8,128)(2,1)}), bf16[576,6144]{1,0:T(8,128)(2,1)}) %all-gather.13.cloned.1.call-update) | async-done | bytes 7077904 | tf_op jit(solution)/shard_map/while/body/eval_jaxpr/all_gather | solution.py:295
  167.6 11.7 fusion.698
  219.6 11.2 fusion.705
  241.5 13.3 %fusion.702 = (f32[3,3,512]{2,1,0:T(4,128)S(1)}, f32[3,1024,512,3]{2,1,3,0:T(8,128)}) fusion(f32[3,1024,512,3]{2,1,3,0:T(8,128)} %get-tuple-element.469, f32[3,3,512]{2,1,0:T(4,128)S(1)} %copy-done.33, pred[512,1024]{0,1:T(8,128)(4,1)S(1)} %fusion.688, bf16[1024,3,64,1]{0,2,3,1:T(8,128)(2,1)S(1)} %bitcast.620, bf16[512,3,3,64]{0,3,2,1:T(8,128)(2,1)S(1)} %bitcast.617), kind=kOutput, calls=%fused_computation.301.clone.1 | convolution fusion | flops 627568128 | bytes 39292928 | tf_op jit(solution)/shard_map/while/body/eval_jaxpr/qkgd,tkd->kgqt/dot_general | solution.py:211
  263.2 13.5 %fusion.703 = bf16[3,3,512,1024]{2,3,1,0:T(8,128)(2,1)S(1)} fusion(f32[3,1024,512,3]{2,1,3,0:T(8,128)} %get-tuple-element.484, f32[3,1024,512,3]{2,1,3,0:T(8,128)} %get-tuple-element.469, f32[3,3,512]{2,1,0:T(4,128)S(1)} %get-tuple-element.485, f32[3,3,512]{2,1,0:T(4,128)S(1)} %copy-done.33, pred[512,1024]{0,1:T(8,128)(4,1)S(1)} %fusion.688), kind=kLoop, calls=%fused_computation.303.clone.1 | loop fusion | flops 28311552 | bytes 47747072 | tf_op jit(solution)/shard_map/while/body/eval_jaxpr/convert_element_type | solution.py:214
  290.8 15.7 %concatenate.101 = f32[576,6144]{1,0:T(8,128)} concatenate(f32[576,960]{1,0:T(8,128)} %fusion.710, f32[576,576]{1,0:T(8,128)} %fusion.711, f32[576,3072]{1,0:T(8,128)} %fusion.712, f32[576,1536]{1,0:T(8,128)} %fusion.713), dimensions={1} | concatenate | bytes 28311552 | tf_op jit(solution)/shard_map/while/body/eval_jaxpr/concatenate | solution.py:246
  306.6 11.6 select_add_fusion.2
  329.3 14.4 %all-gather.4 = bf16[8,72,2]{1,2,0:T(2,128)(2,1)S(1)} all-gather(bf16[1,72,2]{1,2,0:T(2,128)(2,1)S(1)} %bitcast.639), channel_id=1, replica_groups=mesh['dp'=4,'fsdp'=8] {'fsdp'}, dimensions={0}, use_global_device_ids=true | all-gather | bytes 2592 | tf_op jit(solution)/shard_map/while/body/eval_jaxpr/all_gather | solution.py:296
  347.0 90.9 %all-gather.13.cloned.1.call-done = bf16[576,6144]{1,0:T(8,128)(2,1)} async-done(((bf16[72,6144]{1,0:T(8,128)(2,1)}), bf16[576,6144]{1,0:T(8,128)(2,1)}) %all-gather.13.cloned.1.call-update) | async-done | bytes 7077904 | tf_op jit(solution)/shard_map/while/body/eval_jaxpr/all_gather | solution.py:295
  483.2 11.4 fusion.698
  535.1 11.2 fusion.705
  557.0 13.3 %fusion.702 = (f32[3,3,512]{2,1,0:T(4,128)S(1)}, f32[3,1024,512,3]{2,1,3,0:T(8,128)}) fusion(f32[3,1024,512,3]{2,1,3,0:T(8,128)} %get-tuple-element.469, f32[3,3,512]{2,1,0:T(4,128)S(1)} %copy-done.33, pred[512,1024]{0,1:T(8,128)(4,1)S(1)} %fusion.688, bf16[1024,3,64,1]{0,2,3,1:T(8,128)(2,1)S(1)} %bitcast.620, bf16[512,3,3,64]{0,3,2,1:T(8,128)(2,1)S(1)} %bitcast.617), kind=kOutput, calls=%fused_computation.301.clone.1 | convolution fusion | flops 627568128 | bytes 39292928 | tf_op jit(solution)/shard_map/while/body/eval_jaxpr/qkgd,tkd->kgqt/dot_general | solution.py:211
  578.7 13.5 %fusion.703 = bf16[3,3,512,1024]{2,3,1,0:T(8,128)(2,1)S(1)} fusion(f32[3,1024,512,3]{2,1,3,0:T(8,128)} %get-tuple-element.484, f32[3,1024,512,3]{2,1,3,0:T(8,128)} %get-tuple-element.469, f32[3,3,512]{2,1,0:T(4,128)S(1)} %get-tuple-element.485, f32[3,3,512]{2,1,0:T(4,128)S(1)} %copy-done.33, pred[512,1024]{0,1:T(8,128)(4,1)S(1)} %fusion.688), kind=kLoop, calls=%fused_computation.303.clone.1 | loop fusion | flops 28311552 | bytes 47747072 | tf_op jit(solution)/shard_map/while/body/eval_jaxpr/convert_element_type | solution.py:214
  606.3 15.7 %concatenate.101 = f32[576,6144]{1,0:T(8,128)} concatenate(f32[576,960]{1,0:T(8,128)} %fusion.710, f32[576,576]{1,0:T(8,128)} %fusion.711, f32[576,3072]{1,0:T(8,128)} %fusion.712, f32[576,1536]{1,0:T(8,128)} %fusion.713), dimensions={1} | concatenate | bytes 28311552 | tf_op jit(solution)/shard_map/while/body/eval_jaxpr/concatenate | solution.py:246
  622.0 15.6 %select_add_fusion.2 = f32[576,6144]{1,0:T(8,128)} fusion(f32[576,6144]{1,0:T(8,128)} %concatenate.101, f32[576,6144]{1,0:T(8,128)} %get-tuple-element.514, pred[]{:T(512)S(6)} %compare.47), kind=kLoop, calls=%fused_computation.312.clone.1 | loop fusion | flops 7077888 | bytes 42467328 | tf_op jit(solution)/shard_map/while/body/eval_jaxpr/add | solution.py:308
  656.8 232.9 %reduce-scatter.3.cloned.1.call-done = f32[72,6144]{1,0:T(8,128)} async-done(((f32[576,6144]{1,0:T(8,128)}), f32[72,6144]{1,0:T(8,128)}) %reduce-scatter.3.cloned.1.call-update) | async-done | bytes 1769488 | tf_op jit(solution)/shard_map/reduce_scatter | solution.py:319
  889.7 46.3 %all-reduce.5.cloned.1.call-done = f32[72,6144]{1,0:T(8,128)} async-done(((f32[72,6144]{1,0:T(8,128)}), f32[72,6144]{1,0:T(8,128)}) %all-reduce.5.cloned.1.call-update) | async-done | bytes 1769488 | tf_op jit(solution)/shard_map/psum | solution.py:322
  940.5 62.8 %all-gather.9.cloned.1.call-done = f32[576,1536]{1,0:T(8,128)} async-done(((f32[72,1536]{1,0:T(8,128)}), f32[576,1536]{1,0:T(8,128)}) %all-gather.9.cloned.1.call-update) | async-done | bytes 3538960 | tf_op jit(solution)/shard_map/all_gather | solution.py:332
  1003.3 139.0 %conditional.1 = (f32[576,1536]{1,0:T(8,128)S(1)}) conditional(s32[]{:T(128)} %clamp.3, f32[576,1536]{1,0:T(8,128)} %all-gather.9.cloned.1.call-done, f32[576,1536]{1,0:T(8,128)} %all-gather.9.cloned.1.call-done, f32[576,1536]{1,0:T(8,128)} %all-gather.9.cloned.1.call-done, ...), branch_computations={%region_20.25_spmd, %region_25.27_spmd, %region_27.29_spmd, %regio... | conditional | flops 74772799488 | bytes 174001792 | solution.py:335
  1145.0 15.4 %all-reduce.2 = f32[576,2]{0,1:T(2,128)S(1)} all-reduce(f32[576,2]{0,1:T(2,128)S(1)} %copy-done.47), channel_id=3, replica_groups=mesh['dp'=4,'fsdp'=8] {'fsdp'}, use_global_device_ids=true, to_apply=%region_18.19.clone | all-reduce | flops 1152 | bytes 9216
  1160.5 67.7 %psum.15 = f32[72,2]{0,1:T(2,128)S(1)} all-reduce(f32[72,2]{0,1:T(2,128)S(1)} %constant_dynamic-slice_fusion.3), channel_id=1, replica_groups=mesh['dp'=4,'fsdp'=8] {'dp'}, use_global_device_ids=true, to_apply=%region_19.20 | all-reduce | flops 144 | bytes 1152 | tf_op jit(solution)/shard_map/psum | solution.py:322
  1228.8 14.5 %all-gather.1 = f32[8,72,2]{1,2,0:T(2,128)S(1)} all-gather(f32[1,72,2]{1,2,0:T(2,128)S(1)} %bitcast.640), channel_id=1, replica_groups=mesh['dp'=4,'fsdp'=8] {'fsdp'}, dimensions={0}, use_global_device_ids=true | all-gather | bytes 5184 | tf_op jit(solution)/shard_map/all_gather | solution.py:333
  (410 shorter events, 391.6 us)
Async XLA Ops:
  11.2 16.9 %copy-start.43 = (s32[2,1024]{1,0:T(2,128)}, s32[2,1024]{1,0:T(2,128)S(1)}, u32[]{:S(2)}) copy-start(s32[2,1024]{1,0:T(2,128)S(1)} %get-tuple-element.537) | copy-start | bytes 24580 | tf_op jit(solution)/shard_map/while
  11.2 111.1 %all-gather.13.cloned.1.call-start = ((), (), s32[]{:S(2)}) async-start(), calls=%async_computation.5 | async-start | bytes 7962624 | tf_op jit(solution)/shard_map/while/body/eval_jaxpr/all_gather | solution.py:295
  28.0 97.7 %copy-start.41 = (f32[576]{0:T(1024)}, f32[576]{0:T(1024)S(1)}, u32[]{:S(2)}) copy-start(f32[576]{0:T(1024)S(1)} %get-tuple-element.458) | copy-start | bytes 6916 | tf_op jit(solution)/shard_map/while
  28.1 97.7 %copy-start.34 = (f32[1024]{0:T(1024)}, f32[1024]{0:T(1024)S(1)}, u32[]{:S(2)}) copy-start(f32[1024]{0:T(1024)S(1)} %add_rsqrt_fusion.4) | copy-start | bytes 12292 | tf_op jit(solution)/shard_map/while
  28.9 98.3 %copy-start.6 = (f32[1024,32]{0,1:T(8,128)}, f32[1024,32]{0,1:T(8,128)S(1)}, u32[]{:S(2)}) copy-start(f32[1024,32]{0,1:T(8,128)S(1)} %get-tuple-element.463) | copy-start | bytes 393220 | tf_op jit(solution)/shard_map/while
  28.9 98.3 %copy-start.8 = (f32[1024,32]{0,1:T(8,128)}, f32[1024,32]{0,1:T(8,128)S(1)}, u32[]{:S(2)}) copy-start(f32[1024,32]{0,1:T(8,128)S(1)} %get-tuple-element.462) | copy-start | bytes 393220 | tf_op jit(solution)/shard_map/while
  167.6 38.6 %copy-start.18 = (f32[1024,576]{0,1:T(8,128)}, f32[1024,576]{0,1:T(8,128)S(1)}, u32[]{:S(2)}) copy-start(f32[1024,576]{0,1:T(8,128)S(1)} %get-tuple-element.475) | copy-start | bytes 7077892 | tf_op jit(solution)/shard_map/while
  327.8 18.0 %copy-start.43 = (s32[2,1024]{1,0:T(2,128)}, s32[2,1024]{1,0:T(2,128)S(1)}, u32[]{:S(2)}) copy-start(s32[2,1024]{1,0:T(2,128)S(1)} %get-tuple-element.537) | copy-start | bytes 24580 | tf_op jit(solution)/shard_map/while
  327.8 110.1 %all-gather.13.cloned.1.call-start = ((), (), s32[]{:S(2)}) async-start(), calls=%async_computation.5 | async-start | bytes 7962624 | tf_op jit(solution)/shard_map/while/body/eval_jaxpr/all_gather | solution.py:295
  345.6 95.7 %copy-start.41 = (f32[576]{0:T(1024)}, f32[576]{0:T(1024)S(1)}, u32[]{:S(2)}) copy-start(f32[576]{0:T(1024)S(1)} %get-tuple-element.458) | copy-start | bytes 6916 | tf_op jit(solution)/shard_map/while
  345.7 95.7 %copy-start.34 = (f32[1024]{0:T(1024)}, f32[1024]{0:T(1024)S(1)}, u32[]{:S(2)}) copy-start(f32[1024]{0:T(1024)S(1)} %add_rsqrt_fusion.4) | copy-start | bytes 12292 | tf_op jit(solution)/shard_map/while
  346.5 96.3 %copy-start.6 = (f32[1024,32]{0,1:T(8,128)}, f32[1024,32]{0,1:T(8,128)S(1)}, u32[]{:S(2)}) copy-start(f32[1024,32]{0,1:T(8,128)S(1)} %get-tuple-element.463) | copy-start | bytes 393220 | tf_op jit(solution)/shard_map/while
  346.5 96.3 %copy-start.8 = (f32[1024,32]{0,1:T(8,128)}, f32[1024,32]{0,1:T(8,128)S(1)}, u32[]{:S(2)}) copy-start(f32[1024,32]{0,1:T(8,128)S(1)} %get-tuple-element.462) | copy-start | bytes 393220 | tf_op jit(solution)/shard_map/while
  483.1 38.5 %copy-start.18 = (f32[1024,576]{0,1:T(8,128)}, f32[1024,576]{0,1:T(8,128)S(1)}, u32[]{:S(2)}) copy-start(f32[1024,576]{0,1:T(8,128)S(1)} %get-tuple-element.475) | copy-start | bytes 7077892 | tf_op jit(solution)/shard_map/while
  622.0 15.6 %copy-start.20 = (f32[1024,576]{0,1:T(8,128)S(1)}, f32[1024,576]{0,1:T(8,128)}, u32[]{:S(2)}) copy-start(f32[1024,576]{0,1:T(8,128)} %get-tuple-element.495) | copy-start | bytes 7077892 | tf_op jit(solution)/shard_map/while
  656.1 233.5 %reduce-scatter.3.cloned.1.call-start = ((), (), s32[]{:S(2)}) async-start(), calls=%async_computation.1 | async-start | bytes 15925248 | tf_op jit(solution)/shard_map/reduce_scatter | solution.py:319
  656.7 279.3 %copy-start.40 = (f32[72,6144]{1,0:T(8,128)S(1)}, f32[72,6144]{1,0:T(8,128)}, u32[]{:S(2)}) copy-start(f32[72,6144]{1,0:T(8,128)} %param.31) | copy-start | bytes 5308420
  656.7 279.3 %all-reduce.5.cloned.1.call-start = ((), (), s32[]{:S(2)}) async-start(), calls=%async_computation.2 | async-start | bytes 3538944 | tf_op jit(solution)/shard_map/psum | solution.py:322
  889.7 113.6 %all-gather.9.cloned.1.call-start = ((), (), s32[]{:S(2)}) async-start(), calls=%async_computation.3 | async-start | bytes 3981312 | tf_op jit(solution)/shard_map/all_gather | solution.py:332
  940.5 303.7 %all-gather.11.cloned.1.call-start = ((), (), s32[]{:S(2)}) async-start(), calls=%async_computation.4 | async-start | bytes 2211840 | tf_op jit(solution)/shard_map/all_gather | solution.py:341
  1003.3 141.7 %copy-start.47 = (f32[576,2]{0,1:T(2,128)S(1)}, f32[576,2]{0,1:T(2,128)}, u32[]{:S(2)}) copy-start(f32[576,2]{0,1:T(2,128)} %get-tuple-element.254) | copy-start | bytes 13828
  1003.3 224.9 %copy-start.52 = (f32[2,72]{1,0:T(2,128)S(1)}, f32[2,72]{1,0:T(2,128)}, u32[]{:S(2)}) copy-start(f32[2,72]{1,0:T(2,128)} %param.30) | copy-start | bytes 1732
  1003.3 240.2 %copy-start.51 = (f32[2,72]{1,0:T(2,128)S(1)}, f32[2,72]{1,0:T(2,128)}, u32[]{:S(2)}) copy-start(f32[2,72]{1,0:T(2,128)} %param.28) | copy-start | bytes 1732
  1228.8 18.7 %copy-start.50 = (f32[2,72]{1,0:T(2,128)}, f32[2,72]{1,0:T(2,128)S(1)}, u32[]{:S(2)}) copy-start(f32[2,72]{1,0:T(2,128)S(1)} %get-tuple-element.318) | copy-start | bytes 1732
  (96 other events, 536.6 us)
Sparse Core Ops, SparseCore 0:
  14.8 107.4 all-gather.12
  331.4 106.4 all-gather.12
Sparse Core Ops, SparseCore 1:
  660.2 229.4 reduce-scatter.2
  891.9 44.1 all-reduce.4
  940.6 62.7 all-gather.8
  1143.2 78.5 all-gather.10
where the time goes:
time: 1260 us
  waiting for transfers between devices  526 us (42%)
  matrix products  355 us (28%)
  other arithmetic  133 us (11%)
  blocking collectives  125 us (10%)
  local copies, waits for them, and re-layouts  60.4 us (5%)
  loops' own time  38.2 us (3%)
  between operations  16.8 us (1%)
    reduce_scatter x1, waiting for transfers between devices, on_device(): lax.psum_scatter(totals[0], 'fsdp', scatter_dimension=0, tiled=True)  233 us
    all_gather x2, waiting for transfers between devices, micro_step(): lax.all_gather(shard_low, 'fsdp', axis=0, tiled=True)  184 us
    psum x1, blocking collectives, on_device(): summed_weights, summed_gains = lax.psum((shard_weights, shard_gains), 'dp')  67.7 us
    all_gather x1, waiting for transfers between devices, on_device(): lax.all_gather(own_block, 'fsdp', axis=0, tiled=True)  62.8 us
    convert_element_type x4, other arithmetic, backward_pass(): (probs * (d_probs - jnp.sum(d_probs * probs, axis=-1, keepdims=True))).as...  49.4 us
    psum x1, waiting for transfers between devices, on_device(): summed_weights, summed_gains = lax.psum((shard_weights, shard_gains), 'dp')  46.3 us
    dot_general x5, matrix products, orthogonal(): gram = jnp.dot(work, work.T, precision=HIGH)  43.9 us
    dot_general x5, matrix products, orthogonal(): work = COEF_A * work + jnp.dot(poly, work, precision=HIGH)  43.6 us
  transfers between devices with their start and end apart: 6, of which 5 were waited for; matrix products, arithmetic and copies ran while one was open for 1% of the time, Pallas kernels for 0%

commit v1 on v0

v1 whole, which is shorter than its diff:
```python
import functools
import math

import jax
import jax.numpy as jnp
from jax import lax
from jax.experimental import pallas as pl
from jax.experimental.pallas import tpu as pltpu
from jax.sharding import PartitionSpec as P

D = 576
HEADS = 9
KVH = 3
HD = 64
FF = 1536
KV = KVH * HD
QKV = D + 2 * KV
NS_STEPS = 5
WINDOW = 512
SEGMENTS = 8

EPS_NORM = 1e-05
ROPE_BASE = 100000.0
MOMENT = 0.95
LEARN = 0.05
GAIN_LEARN = 0.1
COEF_A = 3.4445
COEF_B = -4.775
COEF_C = 2.0315
F32 = jnp.float32
BF16 = jnp.bfloat16
TQ = 256
TM = 512
FC = 512
VMEM_LIMIT = 60 * 1024 * 1024


def dot(a, b):
    return jnp.dot(a, b, preferred_element_type=F32)


def dot_nt(a, b):
    return lax.dot_general(a, b, (((1,), (1,)), ((), ())), preferred_element_type=F32)


def dot_tn(a, b):
    return lax.dot_general(a, b, (((0,), (0,)), ((), ())), preferred_element_type=F32)


def lane_iota(rows):
    return lax.broadcasted_iota(jnp.int32, (rows, 128), 1)


def swap_pairs(z, lane):
    return jnp.where(lane % 64 < 32, pltpu.roll(z, 96, 1), pltpu.roll(z, 32, 1))


def key_span(tile):
    first = max(0, (tile * TQ - (WINDOW - 1)) // TQ * TQ)
    return first, (tile + 1) * TQ


def mask_bias(start_ref, tile):
    first, stop = key_span(tile)
    width = stop - first
    query = tile * TQ + lax.broadcasted_iota(jnp.int32, (TQ, width), 0)
    key = first + lax.broadcasted_iota(jnp.int32, (TQ, width), 1)
    start = start_ref[tile * TQ : (tile + 1) * TQ, :]
    return jnp.where((key <= query) & (key >= start), 0.0, -1e30).astype(F32)


def place_heads(chunk, lane, take_low):
    other = pltpu.roll(chunk, 64, 1)
    low = chunk if take_low else other
    high = other if take_low else chunk
    return (
        jnp.where(lane < 64, low, 0.0).astype(BF16),
        jnp.where(lane < 64, 0.0, high).astype(BF16),
    )


def place_keys(chunks, lane, kz_ref, vz_ref, rows):
    spots = [(4, False), (5, True), (5, False)], [(6, True), (6, False), (7, True)]
    for ref, spot in zip((kz_ref, vz_ref), spots):
        for head, (chunk, take_low) in enumerate(spot):
            low, high = place_heads(chunks[chunk], lane, take_low)
            ref[0, head, rows, :] = low
            ref[1, head, rows, :] = high


def norm_rows(values):
    return lax.rsqrt(jnp.mean(values * values, axis=-1, keepdims=True) + EPS_NORM)


def attention_fwd_kernel(
    x_ref, cos_ref, sin_ref, start_ref, g1_ref, w_ref, qkv_ref, o_ref, lse_ref, kz_ref, vz_ref
):
    seq = x_ref.shape[0]
    lane = lane_iota(TQ)
    for tile in range(seq // TQ):
        rows = slice(tile * TQ, (tile + 1) * TQ)
        x = x_ref[rows, :].astype(F32)
        a = (x * norm_rows(x) * g1_ref[...]).astype(BF16)
        proj = dot(a, w_ref[...])
        cos, sin = cos_ref[rows, :], sin_ref[rows, :]
        chunks = {}
        for c in range(8):
            z = proj[:, c * 128 : min((c + 1) * 128, QKV)]
            if c == 7:
                z = jnp.concatenate([z, z], axis=1)
            if c < 6:
                z = z * cos + swap_pairs(z, lane) * sin
            if c < 4:
                z = z * 0.125
            if c == 4:
                z = jnp.where(lane < 64, z * 0.125, z)
            chunks[c] = z
            low = z.astype(BF16)
            if c < 7:
                qkv_ref[rows, c * 128 : (c + 1) * 128] = low
            else:
                qkv_ref[rows, c * 128 : QKV] = low[:, :64]
        place_keys(chunks, lane, kz_ref, vz_ref, rows)
    for tile in range(seq // TQ):
        rows = slice(tile * TQ, (tile + 1) * TQ)
        first, stop = key_span(tile)
        bias = mask_bias(start_ref, tile)
        lse = jnp.zeros((TQ, 128), F32)
        for c in range(5):
            q = qkv_ref[rows, c * 128 : (c + 1) * 128]
            out = None
            for half in range(2 if c < 4 else 1):
                head = 2 * c + half
                group = head // (HEADS // KVH)
                s = dot_nt(q, kz_ref[half, group, first:stop, :]) + bias
                top = jnp.max(s, axis=-1, keepdims=True)
                e = jnp.exp(s - top)
                total = jnp.sum(e, axis=-1, keepdims=True)
                p = (e * (1.0 / total)).astype(BF16)
                part = dot(p, vz_ref[half, group, first:stop, :])
                out = part if out is None else out + part
                lse = jnp.where(lane == head, top + jnp.log(total), lse)
            if c < 4:
                o_ref[rows, c * 128 : (c + 1) * 128] = out.astype(BF16)
            else:
                o_ref[rows, c * 128 : D] = out[:, :64].astype(BF16)
        lse_ref[rows, :] = lse


def feed_kernel(
    x_ref, o_ref, dy_ref, g2_ref, wo_ref, wg_ref, wu_ref, wd_ref,
    out_ref, dh2_ref, do_ref, go_ref, gg_ref, gu_ref, gd_ref, dg2_ref,
    acc_o, acc_g, acc_u, acc_d,
):
    step = pl.program_id(0)

    @pl.when(step == 0)
    def _():
        acc_o[...] = jnp.zeros_like(acc_o)
        acc_g[...] = jnp.zeros_like(acc_g)
        acc_u[...] = jnp.zeros_like(acc_u)
        acc_d[...] = jnp.zeros_like(acc_d)
        dg2_ref[...] = jnp.zeros_like(dg2_ref)

    g2 = g2_ref[...]
    o = o_ref[...]
    h2 = x_ref[...].astype(F32) + dot(o, wo_ref[...])
    r2 = norm_rows(h2)
    u2 = h2 * r2
    b = (u2 * g2).astype(BF16)
    dm = dy_ref[...]
    result = h2
    db = jnp.zeros_like(h2)
    for c in range(FF // FC):
        cols = slice(c * FC, (c + 1) * FC)
        wg, wu, wd = wg_ref[:, cols], wu_ref[:, cols], wd_ref[:, cols]
        gate = dot(b, wg)
        up = dot(b, wu)
        dinner = dot(dm, wd)
        sig = 0.5 + 0.5 * jnp.tanh(0.5 * gate)
        silu = gate * sig
        inner = (silu * up).astype(BF16)
        dgate = (dinner * up * (sig + silu * (1.0 - sig))).astype(BF16)
        dup = (dinner * silu).astype(BF16)
        result = result + dot_nt(inner, wd)
        acc_d[:, cols] += dot_tn(dm, inner)
        db = db + dot_nt(dgate, wg) + dot_nt(dup, wu)
        acc_g[:, cols] += dot_tn(b, dgate)
        acc_u[:, cols] += dot_tn(b, dup)
    out_ref[...] = result.astype(BF16)
    dg2_ref[...] += jnp.sum(db * u2, axis=0, keepdims=True)
    e2 = db * g2
    dh2 = r2 * (e2 - u2 * jnp.mean(e2 * u2, axis=-1, keepdims=True)) + dm.astype(F32)
    dh2_ref[...] = dh2
    dattn = dh2.astype(BF16)
    acc_o[...] += dot_tn(o, dattn)
    do_ref[...] = dot_nt(dattn, wo_ref[...]).astype(BF16)

    @pl.when(step == pl.num_programs(0) - 1)
    def _():
        go_ref[...] = acc_o[...].astype(BF16)
        gg_ref[...] = acc_g[...].astype(BF16)
        gu_ref[...] = acc_u[...].astype(BF16)
        gd_ref[...] = acc_d[...].astype(BF16)


def attention_bwd_kernel(
    x_ref, cos_ref, sin_ref, start_ref, g1_ref, w_ref, qkv_ref, o_ref, lse_ref, do_ref, dh2_ref,
    dx_ref, gq_ref, dg1_ref,
    kz_ref, vz_ref, kvt_ref, dq_ref, acc,
):
    seq = x_ref.shape[0]
    lane = lane_iota(TQ)

    @pl.when(pl.program_id(0) == 0)
    def _():
        acc[...] = jnp.zeros_like(acc)
        dg1_ref[...] = jnp.zeros_like(dg1_ref)

    for tile in range(seq // TQ):
        rows = slice(tile * TQ, (tile + 1) * TQ)
        chunks = {}
        for c in range(4, 8):
            z = qkv_ref[rows, c * 128 : min((c + 1) * 128, QKV)].astype(F32)
            if c == 7:
                z = jnp.concatenate([z, z], axis=1)
            chunks[c] = z
        place_keys(chunks, lane, kz_ref, vz_ref, rows)
    kvt_ref[...] = jnp.zeros_like(kvt_ref)
    for tile in range(seq // TQ):
        rows = slice(tile * TQ, (tile + 1) * TQ)
        first, stop = key_span(tile)
        bias = mask_bias(start_ref, tile)
        lse = lse_ref[rows, :]
        cos, sin = cos_ref[rows, :], sin_ref[rows, :]
        for c in range(5):
            wide = slice(c * 128, (c + 1) * 128)
            q = qkv_ref[rows, wide]
            if c < 4:
                do = do_ref[rows, wide]
                o = o_ref[rows, wide]
            else:
                do = do_ref[rows, c * 128 : D]
                do = jnp.concatenate([do, do], axis=1)
                o = o_ref[rows, c * 128 : D]
                o = jnp.concatenate([o, o], axis=1)
            prod = do.astype(F32) * o.astype(F32)
            dq = None
            for half in range(2 if c < 4 else 1):
                head = 2 * c + half
                group = head // (HEADS // KVH)
                mine = lane < 64 if half == 0 else lane >= 64
                delta = jnp.sum(jnp.where(mine, prod, 0.0), axis=-1, keepdims=True)
                kz = kz_ref[half, group, first:stop, :]
                s = dot_nt(q, kz) + bias
                p = jnp.exp(s - lse[:, head : head + 1])
                dp = dot_nt(do, vz_ref[half, group, first:stop, :])
                ds = (p * (dp - delta)).astype(BF16)
                pl_ = p.astype(BF16)
                part = dot(ds, kz)
                dq = part if dq is None else dq + part
                own = slice(half * 64, half * 64 + 64)
                krow = 64 + group * 64
                vrow = 256 + group * 64
                kvt_ref[krow : krow + 64, first:stop] += dot_tn(q, ds)[own, :]
                kvt_ref[vrow : vrow + 64, first:stop] += dot_tn(do, pl_)[own, :]
            dq = dq * 0.125
            dq = dq * cos - swap_pairs(dq, lane) * sin
            dq_ref[rows, wide] = dq.astype(BF16)
    for tile in range(seq // TQ):
        rows = slice(tile * TQ, (tile + 1) * TQ)
        cos, sin = cos_ref[rows, :], sin_ref[rows, :]
        for c in range(4):
            z = kvt_ref[c * 128 : (c + 1) * 128, rows].T
            if c < 2:
                z = z * cos - swap_pairs(z, lane) * sin
            z = z.astype(BF16)
            if c == 0:
                z = jnp.where(lane < 64, dq_ref[rows, 512:640].astype(F32), z.astype(F32)).astype(BF16)
            wide = slice(512 + c * 128, 512 + (c + 1) * 128)
            dq_ref[rows, wide] = z
        x = x_ref[rows, :].astype(F32)
        g1 = g1_ref[...]
        r1 = norm_rows(x)
        u1 = x * r1
        a = (u1 * g1).astype(BF16)
        dqkv = dq_ref[rows, 0:QKV]
        acc[...] += dot_tn(a, dqkv)
        da = dot_nt(dqkv, w_ref[...])
        dg1_ref[...] += jnp.sum(da * u1, axis=0, keepdims=True)
        e1 = da * g1
        dx_ref[rows, :] = r1 * (e1 - u1 * jnp.mean(e1 * u1, axis=-1, keepdims=True)) + dh2_ref[rows, :]

    @pl.when(pl.program_id(0) == pl.num_programs(0) - 1)
    def _():
        gq_ref[...] = acc[...].astype(BF16)


def whole(shape):
    zeros = (0,) * len(shape)
    return pl.BlockSpec(shape, lambda *_: zeros, pipeline_mode=pl.Buffered(1))


def per_seq(width, seq):
    return pl.BlockSpec((None, seq, width), lambda s: (s, 0, 0))


def attention_fwd(x, cos, sin, start, g1, w):
    count, seq, _ = x.shape
    return pl.pallas_call(
        attention_fwd_kernel,
        grid=(count,),
        in_specs=[
            per_seq(D, seq), per_seq(128, seq), per_seq(128, seq), per_seq(1, seq),
            whole((1, D)), whole((D, QKV)),
        ],
        out_specs=[per_seq(QKV, seq), per_seq(D, seq), per_seq(128, seq)],
        out_shape=[
            jax.ShapeDtypeStruct((count, seq, QKV), BF16),
            jax.ShapeDtypeStruct((count, seq, D), BF16),
            jax.ShapeDtypeStruct((count, seq, 128), F32),
        ],
        scratch_shapes=[
            pltpu.VMEM((2, KVH, seq, 128), BF16),
            pltpu.VMEM((2, KVH, seq, 128), BF16),
        ],
        compiler_params=pltpu.CompilerParams(vmem_limit_bytes=VMEM_LIMIT),
        cost_estimate=pl.CostEstimate(
            flops=count * 30_000_000_000, bytes_accessed=count * 10_000_000, transcendentals=0
        ),
        name="attention_fwd",
    )(x, cos, sin, start, g1, w)


def feed(x, o, dy, g2, wo, wg, wu, wd):
    tokens = x.shape[0]
    tile = min(TM, tokens)

    def rows(width):
        return pl.BlockSpec((tile, width), lambda t: (t, 0))

    return pl.pallas_call(
        feed_kernel,
        grid=(tokens // tile,),
        in_specs=[rows(D), rows(D), rows(D), whole((1, D)), whole((D, D))]
        + [whole((D, FF))] * 3,
        out_specs=[rows(D), rows(D), rows(D), whole((D, D))] + [whole((D, FF))] * 3 + [whole((1, D))],
        out_shape=[
            jax.ShapeDtypeStruct((tokens, D), BF16),
            jax.ShapeDtypeStruct((tokens, D), F32),
            jax.ShapeDtypeStruct((tokens, D), BF16),
            jax.ShapeDtypeStruct((D, D), BF16),
            jax.ShapeDtypeStruct((D, FF), BF16),
            jax.ShapeDtypeStruct((D, FF), BF16),
            jax.ShapeDtypeStruct((D, FF), BF16),
            jax.ShapeDtypeStruct((1, D), F32),
        ],
        scratch_shapes=[pltpu.VMEM((D, D), F32)] + [pltpu.VMEM((D, FF), F32)] * 3,
        compiler_params=pltpu.CompilerParams(vmem_limit_bytes=VMEM_LIMIT),
        cost_estimate=pl.CostEstimate(
            flops=tokens * 18_000_000, bytes_accessed=30_000_000, transcendentals=0
        ),
        name="feed",
    )(x, o, dy, g2, wo, wg, wu, wd)


def attention_bwd(x, cos, sin, start, g1, w, qkv, o, lse, do, dh2):
    count, seq, _ = x.shape
    return pl.pallas_call(
        attention_bwd_kernel,
        grid=(count,),
        in_specs=[
            per_seq(D, seq), per_seq(128, seq), per_seq(128, seq), per_seq(1, seq),
            whole((1, D)), whole((D, QKV)),
            per_seq(QKV, seq), per_seq(D, seq), per_seq(128, seq), per_seq(D, seq), per_seq(D, seq),
        ],
        out_specs=[per_seq(D, seq), whole((D, QKV)), whole((1, D))],
        out_shape=[
            jax.ShapeDtypeStruct((count, seq, D), F32),
            jax.ShapeDtypeStruct((D, QKV), BF16),
            jax.ShapeDtypeStruct((1, D), F32),
        ],
        scratch_shapes=[
            pltpu.VMEM((2, KVH, seq, 128), BF16),
            pltpu.VMEM((2, KVH, seq, 128), BF16),
            pltpu.VMEM((512, seq), F32),
            pltpu.VMEM((seq, 1024), BF16),
            pltpu.VMEM((D, QKV), F32),
        ],
        compiler_params=pltpu.CompilerParams(vmem_limit_bytes=VMEM_LIMIT),
        cost_estimate=pl.CostEstimate(
            flops=count * 50_000_000_000, bytes_accessed=count * 12_000_000, transcendentals=0
        ),
        name="attention_bwd",
    )(x, cos, sin, start, g1, w, qkv, o, lse, do, dh2)


def sweep(work, scale, shift):
    low = work.astype(BF16)
    size = work.shape[0]
    gram = dot_nt(low, low)
    if shift:
        eye = lax.broadcasted_iota(jnp.int32, (size, size), 0) == lax.broadcasted_iota(
            jnp.int32, (size, size), 1
        )
        gram = gram - jnp.where(eye, shift, 0.0)
    glow = gram.astype(BF16)
    poly = (COEF_B + 2 * COEF_C * shift) * gram + COEF_C * dot(glow, glow)
    return (COEF_A + COEF_B * shift + COEF_C * shift * shift) * work + dot(poly.astype(BF16), low)


def orthogonalize_kernel(shifts, scale, x_ref, out_ref):
    work = x_ref[...].astype(F32)
    work = work * (1.0 / (jnp.sqrt(jnp.sum(work * work)) + 1e-07))
    out_ref[...] = work
    for shift in shifts:
        out_ref[...] = sweep(out_ref[...], scale, shift)
    out_ref[...] = out_ref[...] * scale


def orthogonalize(block):
    rows, cols = block.shape
    if rows > cols:
        return orthogonalize(block.T).T
    shifts = (0.0, 0.0, 0.8, 0.8, 0.8) if rows <= 256 else (0.0, 0.0, 0.0, 0.8, 0.8)
    return pl.pallas_call(
        functools.partial(orthogonalize_kernel, shifts, 0.2 * math.sqrt(max(rows, cols))),
        out_shape=jax.ShapeDtypeStruct((rows, cols), F32),
        compiler_params=pltpu.CompilerParams(vmem_limit_bytes=VMEM_LIMIT),
        name="orthogonalize",
    )(block)


def attention_block(block):
    bounds = [0, D, D + KV, D + 2 * KV, FF]
    pieces = [orthogonalize(block[:, bounds[i] : bounds[i + 1]]) for i in range(4)]
    return jnp.concatenate(pieces, axis=1)


def rope_tables(seg):
    count, seq = seg.shape
    start = jnp.zeros_like(seg)
    for value in range(1, SEGMENTS):
        before = jnp.sum((seg < value).astype(jnp.int32), axis=1, keepdims=True)
        start = jnp.where(seg == value, before, start)
    offset = (jnp.arange(seq, dtype=jnp.int32)[None, :] - start).astype(F32)
    inverse = 1.0 / ROPE_BASE ** (jnp.arange(0, HD, 2, dtype=F32) / HD)
    angle = offset[:, :, None] * inverse[None, None, :]
    cos, sin = jnp.cos(angle), jnp.sin(angle)
    return (
        start[:, :, None],
        jnp.concatenate([cos, cos, cos, cos], axis=-1),
        jnp.concatenate([-sin, sin, -sin, sin], axis=-1),
    )


def layer_pass(x, seg, dy, gains, w_qkv, w_o, w_g, w_u, w_d):
    count, seq, _ = x.shape
    start, cos, sin = rope_tables(seg)
    g1, g2 = gains[0:1], gains[1:2]
    qkv, o, lse = attention_fwd(x, cos, sin, start, g1, w_qkv)
    flat = lambda v: v.reshape(count * seq, v.shape[-1])
    deep = lambda v: v.reshape(count, seq, v.shape[-1])
    out, dh2, do, go, gg, gu, gd, dg2 = feed(flat(x), flat(o), flat(dy), g2, w_o, w_g, w_u, w_d)
    dx, gq, dg1 = attention_bwd(x, cos, sin, start, g1, w_qkv, qkv, o, lse, deep(do), deep(dh2))
    return deep(out), dx, (gq, go, gg, gu, gd), jnp.concatenate([dg1, dg2], axis=0)


def on_device(hidden_in, seg_ids, out_grad, gains, matrices, gain_momentum, mat_momentum):
    shard_rows = matrices.shape[0]
    total_cols = matrices.shape[1]
    count, local, seq, _ = hidden_in.shape
    total_tokens = count * local * seq * lax.axis_size("dp") * lax.axis_size("fsdp")
    grad_scale = float(total_tokens) ** (-0.5)
    shard_low = matrices.astype(BF16)
    cuts = [0, QKV, FF, 2 * FF, 3 * FF, 4 * FF]
    gather = lambda v: lax.all_gather(v, "fsdp", axis=0, tiled=True)
    w_qkv = gather(shard_low[:, :QKV])
    gain_pair = gather(gains.T.astype(BF16)).astype(F32).T
    w_o = gather(shard_low[:, QKV:FF])
    w_g, w_u, w_d = (gather(shard_low[:, cuts[i] : cuts[i + 1]]) for i in (2, 3, 4))
    x = hidden_in.reshape(count * local, seq, D)
    dy = out_grad.reshape(count * local, seq, D)
    seg = seg_ids.reshape(count * local, seq)
    out, dx, grads, gain_grads = layer_pass(x, seg, dy, gain_pair, w_qkv, w_o, w_g, w_u, w_d)
    shards = [lax.psum_scatter(g, "fsdp", scatter_dimension=0, tiled=True) for g in grads]
    summed = lax.psum(jnp.concatenate(shards, axis=1).astype(F32), "dp")
    summed_gains = lax.psum(
        lax.psum_scatter(gain_grads.T, "fsdp", scatter_dimension=0, tiled=True), "dp"
    )
    matrix_grad = summed * grad_scale
    gain_grad = (summed_gains * grad_scale).T
    new_mat_momentum = MOMENT * mat_momentum + matrix_grad
    new_gain_momentum = MOMENT * gain_momentum + gain_grad
    look = matrix_grad + MOMENT * new_mat_momentum
    owner_group = lax.axis_index("dp")
    block_cols = total_cols // 4
    own_block = lax.dynamic_slice_in_dim(look, owner_group * block_cols, block_cols, 1)
    whole_block = gather(own_block.astype(BF16))
    whole_gain_mom = gather(new_gain_momentum.T)
    orthogonal_block = lax.cond(owner_group == 0, attention_block, orthogonalize, whole_block)
    own_rows = lax.dynamic_slice_in_dim(
        orthogonal_block, lax.axis_index("fsdp") * shard_rows, shard_rows, 0
    )
    update_rows = lax.all_gather(own_rows.astype(BF16), "dp", axis=1, tiled=True).astype(F32)
    new_matrices = matrices - LEARN * update_rows
    spread = lax.rsqrt(jnp.mean(whole_gain_mom * whole_gain_mom, axis=0, keepdims=True) + 1e-06)
    new_gains = gains - GAIN_LEARN * new_gain_momentum * spread.T
    return (
        out.reshape(hidden_in.shape),
        dx.reshape(hidden_in.shape),
        matrix_grad,
        gain_grad,
        new_mat_momentum,
        new_gain_momentum,
        new_matrices,
        new_gains,
    )


def solution(mesh):
    in_specs = (
        P(None, ("dp", "fsdp"), None, None),
        P(None, ("dp", "fsdp"), None),
        P(None, ("dp", "fsdp"), None, None),
        P(None, "fsdp"),
        P("fsdp", None),
        P(None, "fsdp"),
        P("fsdp", None),
    )
    out_specs = (
        P(None, ("dp", "fsdp"), None, None),
        P(None, ("dp", "fsdp"), None, None),
        P("fsdp", None),
        P(None, "fsdp"),
        P("fsdp", None),
        P(None, "fsdp"),
        P("fsdp", None),
        P(None, "fsdp"),
    )
    return jax.shard_map(
        on_device, mesh=mesh, in_specs=in_specs, out_specs=out_specs, check_vma=False
    )
```

time: 1260 us -> 766 us (0.61)
  matrix products: 355 us -> 0 us
  Pallas kernels: 0 us -> 166 us
  waiting for transfers between devices: 526 us -> 376 us
  other arithmetic: 133 us -> 20.8 us
  local copies, waits for them, and re-layouts: 60.4 us -> 27.3 us
  loops' own time: 38.2 us -> 8.89 us
  blocking collectives: 125 us -> 142 us
    dot_general x63 -> x0, matrix products: 355 us -> none  [the longest x5 43.9 us: orthogonal(): gram = jnp.dot(work, work.T, precision=HIGH)]
    pallas_call x0 -> x4, Pallas kernels: none -> 166 us  [the longest x1 59.2 us: feed(): pl.pallas_call(feed_kernel, grid=(tokens // tile,), in_specs=[rows(D), ro...]
    all_gather x4 -> x5, waiting for transfers between devices: 247 us -> 101 us  [on_device(): gather = lambda v: lax.all_gather(v, 'fsdp', axis=0, tiled=True)]
    convert_element_type x8 -> x3, other arithmetic: 51.8 us -> 2.39 us  [the longest x1 1.57 us: on_device(): shard_low = matrices.astype(BF16)]
    all_gather x3 -> x4, blocking collectives: 42.4 us -> 89.2 us  [the longest x3 57.2 us: on_device(): gather = lambda v: lax.all_gather(v, 'fsdp', axis=0, tiled=True)]
    psum x1 -> x0, waiting for transfers between devices: 46.3 us -> none  [on_device(): summed_weights, summed_gains = lax.psum((shard_weights, shard_gains), 'dp')]
    reduce_scatter x1 -> x4, waiting for transfers between devices: 233 us -> 271 us  [on_device(): lax.psum_scatter(g, 'fsdp', scatter_dimension=0, tiled=True)]
    add x13 -> x0, other arithmetic: 33 us -> none  [the longest x4 27.2 us: micro_step(): running = (running[0] + grad_weights, running[1] + grad_gains.T)]
  transfers between devices with their start and end apart: 6 -> 10, of which waited for: 5 -> 7; matrix products, arithmetic and copies ran while one was open for 1% -> 5% of each run, Pallas kernels for 0% -> 11%
where the time goes in v1:
time: 766 us; the launch traced here: 757 us
  waiting for transfers between devices  376 us (49%)
  Pallas kernels  166 us (22%)
  blocking collectives  142 us (19%)
  local copies, waits for them, and re-layouts  27.3 us (4%)
  other arithmetic  20.8 us (3%)
  between operations  15.3 us (2%)
  loops' own time  8.89 us (1%)
    reduce_scatter x4, waiting for transfers between devices, on_device(): lax.psum_scatter(g, 'fsdp', scatter_dimension=0, tiled=True)  271 us
    all_gather x5, waiting for transfers between devices, on_device(): gather = lambda v: lax.all_gather(v, 'fsdp', axis=0, tiled=True)  101 us
    pallas_call x1, Pallas kernels, feed(): pl.pallas_call(feed_kernel, grid=(tokens // tile,), in_specs=[rows(D), ro...  59.2 us
    all_gather x3, blocking collectives, on_device(): gather = lambda v: lax.all_gather(v, 'fsdp', axis=0, tiled=True)  57.2 us
    pallas_call x1, Pallas kernels, attention_bwd(): pl.pallas_call(attention_bwd_kernel, grid=(count,), in_specs=[per_seq(D,...  46.2 us
    psum x1, blocking collectives, on_device(): summed = lax.psum(jnp.concatenate(shards, axis=1).astype(F32), 'dp')  37.9 us
    pallas_call x1, Pallas kernels, attention_fwd(): pl.pallas_call(attention_fwd_kernel, grid=(count,), in_specs=[per_seq(D,...  36.4 us
    all_gather x1, blocking collectives, on_device(): lax.all_gather(own_rows.astype(BF16), 'dp', axis=1, tiled=True).astype(F32)  31.9 us
  transfers between devices with their start and end apart: 10, of which 7 were waited for; matrix products, arithmetic and copies ran while one was open for 5% of the time, Pallas kernels for 11%

profile of v1, /device:TPU:7, one launch (start us, length us, event | category | flops | bytes accessed | tf_op | source)
XLA Modules:
  0.0 756.7 jit_solution(18318149519879393379)
XLA Ops:
  18.6 2.6 copy.287
  21.2 13.4 %all-gather = bf16[8,72,2]{1,2,0:T(2,128)(2,1)S(1)} all-gather(bf16[1,72,2]{1,2,0:T(2,128)(2,1)S(1)} %convert_bitcast_fusion), channel_id=1, replica_groups=mesh['dp'=4,'fsdp'=8] {'fsdp'}, dimensions={0}, use_global_device_ids=true | all-gather | bytes 2592 | tf_op jit(solution)/shard_map/all_gather | solution.py:477
  35.3 29.7 %all_gather.35.wo_ref = bf16[576,576]{1,0:T(8,128)(2,1)} all-gather(bf16[72,576]{1,0:T(8,128)(2,1)S(1)} %copy-done.9), channel_id=1, replica_groups=mesh['dp'=4,'fsdp'=8] {'fsdp'}, dimensions={0}, use_global_device_ids=true | all-gather | bytes 746496 | tf_op jit(solution)/shard_map/all_gather | solution.py:477
  64.9 4.4 copy.309
  69.5 3.7 fusion.1
  73.2 3.0 pad_maximum_fusion
  78.0 36.4 %attention_fwd.1 = (bf16[2,1024,960]{2,1,0:T(8,128)(2,1)}, bf16[2,1024,576]{2,1,0:T(8,128)(2,1)}, f32[2,1024,128]{2,1,0:T(8,128)}) custom-call(bf16[2,1024,576]{2,1,0:T(8,128)(2,1)} %bitcast.76, f32[2,1024,128]{2,1,0:T(8,128)} %get-tuple-element.153.cos_ref, f32[2,1024,128]{2,1,0:T(8,128)} %get-tuple-element.154.sin_ref, ...), custom_call_target="tpu_custom_call" | custom-call | flops 60000002048 | bytes 20000000 | tf_op jit(solution)/shard_map/attention_fwd/pallas_call | solution.py:310
  114.4 35.0 %all-gather.12.cloned.1.call-done.wu_ref = bf16[576,1536]{1,0:T(8,128)(2,1)} async-done(((bf16[72,1536]{1,0:T(8,128)(2,1)}), bf16[576,1536]{1,0:T(8,128)(2,1)}) %all-gather.12.cloned.1.call-update) | async-done | bytes 1769488 | tf_op jit(solution)/shard_map/all_gather | solution.py:477
  149.4 47.1 %all-gather.14.cloned.1.call-done.wd_ref = bf16[576,1536]{1,0:T(8,128)(2,1)} async-done(((bf16[72,1536]{1,0:T(8,128)(2,1)}), bf16[576,1536]{1,0:T(8,128)(2,1)}) %all-gather.14.cloned.1.call-update) | async-done | bytes 1769488 | tf_op jit(solution)/shard_map/all_gather | solution.py:477
  196.5 59.2 %feed.1 = (bf16[2048,576]{1,0:T(8,128)(2,1)}, f32[2048,576]{1,0:T(8,128)}, bf16[2048,576]{1,0:T(8,128)(2,1)}, bf16[576,576]{1,0:T(8,128)(2,1)}, bf16[576,1536]{1...) custom-call(bf16[2048,576]{1,0:T(8,128)(2,1)} %bitcast.77, ...), custom_call_target="tpu_custom_call" | custom-call | flops 36864000000 | bytes 30000000 | tf_op jit(solution)/shard_map/feed/pallas_call | solution.py:342
  255.8 46.2 %attention_bwd.1 = (f32[2,1024,576]{2,1,0:T(8,128)}, bf16[576,960]{1,0:T(8,128)(2,1)}, f32[1,576]{1,0:T(1,128)}) custom-call(bf16[2,1024,576]{2,1,0:T(8,128)(2,1)} %bitcast.78, f32[2,1024,128]{2,1,0:T(8,128)} %get-tuple-element.153.cos_ref, f32[2,1024,128]{2,1,0:T(8,128)} %get-tuple-element.154.sin_ref, s32[2,1024,1]{2,1,0:T(8,128)} %select_select_fusion.start_ref, ...), custom_call_target="tpu_custom_call" | custom-call | flops 99999997952 | bytes 24000000 | tf_op jit(solution)/shard_map/attention_bwd/pallas_call | solution.py:369
  305.7 15.3 %all-reduce.1 = f32[576,2]{0,1:T(2,128)S(1)} all-reduce(f32[576,2]{0,1:T(2,128)S(1)} %maximum_bitcast_fusion), channel_id=7, replica_groups=mesh['dp'=4,'fsdp'=8] {'fsdp'}, use_global_device_ids=true, to_apply=%region_13.14.clone | all-reduce | flops 1152 | bytes 9216
  321.0 62.4 %reduce-scatter.9.cloned.1.call-done = bf16[72,960]{1,0:T(8,128)(2,1)} async-done(((bf16[576,960]{1,0:T(8,128)(2,1)}), bf16[72,960]{1,0:T(8,128)(2,1)}) %reduce-scatter.9.cloned.1.call-update) | async-done | bytes 138256 | tf_op jit(solution)/shard_map/reduce_scatter | solution.py:486
  383.4 69.6 %reduce-scatter.11.cloned.1.call-done = bf16[72,1536]{1,0:T(8,128)(2,1)} async-done(((bf16[576,1536]{1,0:T(8,128)(2,1)}), bf16[72,1536]{1,0:T(8,128)(2,1)}) %reduce-scatter.11.cloned.1.call-update) | async-done | bytes 221200 | tf_op jit(solution)/shard_map/reduce_scatter | solution.py:486
  453.0 69.5 %reduce-scatter.13.cloned.1.call-done = bf16[72,1536]{1,0:T(8,128)(2,1)} async-done(((bf16[576,1536]{1,0:T(8,128)(2,1)}), bf16[72,1536]{1,0:T(8,128)(2,1)}) %reduce-scatter.13.cloned.1.call-update) | async-done | bytes 221200 | tf_op jit(solution)/shard_map/reduce_scatter | solution.py:486
  522.5 69.6 %reduce-scatter.15.cloned.1.call-done = bf16[72,1536]{1,0:T(8,128)(2,1)} async-done(((bf16[576,1536]{1,0:T(8,128)(2,1)}), bf16[72,1536]{1,0:T(8,128)(2,1)}) %reduce-scatter.15.cloned.1.call-update) | async-done | bytes 221200 | tf_op jit(solution)/shard_map/reduce_scatter | solution.py:486
  593.5 37.9 %all-reduce.4 = (f32[72,6144]{1,0:T(8,128)}, f32[72,2]{0,1:T(2,128)S(1)}) all-reduce(bf16[72,6144]{1,0:T(8,128)(2,1)S(1)} %concatenate.17, f32[72,2]{0,1:T(2,128)S(1)} %constant_dynamic-slice_fusion), channel_id=1, replica_groups=mesh['dp'=4,'fsdp'=8] {'dp'}, use_global_device_ids=true, to_apply=%region_12.13 | all-reduce | flops 442512 | bytes 2655360 | tf_op jit(solution)/shard_map/psum | solution.py:487
  635.8 5.9 copy.311
  644.7 14.2 %all-gather.1 = f32[8,72,2]{1,2,0:T(2,128)S(1)} all-gather(f32[1,72,2]{1,2,0:T(2,128)S(1)} %bitcast.85), channel_id=1, replica_groups=mesh['dp'=4,'fsdp'=8] {'fsdp'}, dimensions={0}, use_global_device_ids=true | all-gather | bytes 5184 | tf_op jit(solution)/shard_map/all_gather | solution.py:477
  659.7 19.1 %all-gather.16.cloned.1.call-done = bf16[576,1536]{1,0:T(8,128)(2,1)} async-done(((bf16[72,1536]{1,0:T(8,128)(2,1)}), bf16[576,1536]{1,0:T(8,128)(2,1)}) %all-gather.16.cloned.1.call-update) | async-done | bytes 1769488 | tf_op jit(solution)/shard_map/all_gather | solution.py:477
  678.8 36.5 %conditional.1 = (bf16[576,1536]{1,0:T(8,128)(2,1)}) conditional(s32[]{:T(128)} %convert_element_type.72, bf16[576,1536]{1,0:T(8,128)(2,1)} %all-gather.16.cloned.1.call-done, bf16[576,1536]{1,0:T(8,128)(2,1)} %all-gather.16.cloned.1.call-done), branch_computations={%region_15.16_spmd, %region_16.17_spmd} | conditional | flops 884736 | bytes 15925284 | solution.py:501
  679.0 24.2 %orthogonalize.5 = f32[576,1536]{1,0:T(8,128)} custom-call(bf16[576,1536]{1,0:T(8,128)(2,1)} %x_ref), custom_call_target="tpu_custom_call" | custom-call | tf_op jit(solution)/shard_map/cond/branch_0_fun/orthogonalize/pallas_call | solution.py:426
  703.2 3.4 convert.1
  716.3 31.9 %all_gather.40 = bf16[72,6144]{1,0:T(8,128)(2,1)S(1)} all-gather(bf16[72,1536]{1,0:T(8,128)(2,1)S(1)} %dynamic-slice_convert_fusion), channel_id=1, replica_groups=mesh['dp'=4,'fsdp'=8] {'dp'}, dimensions={1}, use_global_device_ids=true | all-gather | bytes 1105920 | tf_op jit(solution)/shard_map/all_gather | solution.py:505
  (99 shorter events, 28.9 us)
Async XLA Ops:
  7.2 70.8 %all-gather.8.cloned.1.call-start = ((), (), s32[]{:S(2)}) async-start(), calls=%async_computation.5 | async-start | bytes 1327104 | tf_op jit(solution)/shard_map/all_gather | solution.py:477
  8.8 3.0 copy-start.10
  9.5 9.1 %copy-start.5 = (bf16[2,1,1024,576]{2,3,1,0:T(8,128)(2,1)S(1)}, bf16[2,1,1024,576]{2,3,1,0:T(8,128)(2,1)}, u32[]{:S(2)}) copy-start(bf16[2,1,1024,576]{2,3,1,0:T(8,128)(2,1)} %param.9) | copy-start | bytes 7077892
  9.5 104.9 %all-gather.10.cloned.1.call-start = ((), (), s32[]{:S(2)}) async-start(), calls=%async_computation.6 | async-start | bytes 1990656 | tf_op jit(solution)/shard_map/all_gather | solution.py:477
  10.4 139.0 %all-gather.12.cloned.1.call-start = ((), (), s32[]{:S(2)}) async-start(), calls=%async_computation.7 | async-start | bytes 1990656 | tf_op jit(solution)/shard_map/all_gather | solution.py:477
  11.2 185.4 %all-gather.14.cloned.1.call-start = ((), (), s32[]{:S(2)}) async-start(), calls=%async_computation.8 | async-start | bytes 1990656 | tf_op jit(solution)/shard_map/all_gather | solution.py:477
  11.7 309.3 %reduce-scatter.17.cloned.1.call-start = ((), (), s32[]{:S(2)}) async-start(), calls=%async_computation.14 | async-start | bytes 829440
  18.6 16.6 %copy-start.9 = (bf16[72,576]{1,0:T(8,128)(2,1)S(1)}, bf16[72,576]{1,0:T(8,128)(2,1)}, u32[]{:S(2)}) copy-start(bf16[72,576]{1,0:T(8,128)(2,1)} %slice.43) | copy-start | bytes 248836
  64.9 4.4 copy-start.12
  64.9 4.4 copy-start.13
  64.9 4.4 copy-start.14
  64.9 4.5 copy-start.20
  73.2 3.0 copy-start.7
  73.2 3.0 copy-start.8
  255.8 127.6 %reduce-scatter.9.cloned.1.call-start = ((), (), s32[]{:S(2)}) async-start(), calls=%async_computation.9 | async-start | bytes 1327104 | tf_op jit(solution)/shard_map/reduce_scatter | solution.py:486
  302.1 150.9 %reduce-scatter.11.cloned.1.call-start = ((), (), s32[]{:S(2)}) async-start(), calls=%async_computation.10 | async-start | bytes 1990656 | tf_op jit(solution)/shard_map/reduce_scatter | solution.py:486
  302.8 219.6 %reduce-scatter.13.cloned.1.call-start = ((), (), s32[]{:S(2)}) async-start(), calls=%async_computation.11 | async-start | bytes 1990656 | tf_op jit(solution)/shard_map/reduce_scatter | solution.py:486
  303.6 288.4 %reduce-scatter.15.cloned.1.call-start = ((), (), s32[]{:S(2)}) async-start(), calls=%async_computation.12 | async-start | bytes 1990656 | tf_op jit(solution)/shard_map/reduce_scatter | solution.py:486
  304.3 327.1 %copy-start.6 = (f32[72,6144]{1,0:T(8,128)S(1)}, f32[72,6144]{1,0:T(8,128)}, u32[]{:S(2)}) copy-start(f32[72,6144]{1,0:T(8,128)} %param.15) | copy-start | bytes 5308420
  304.3 374.5 %all-gather.16.cloned.1.call-start = ((), (), s32[]{:S(2)}) async-start(), calls=%async_computation.13 | async-start | bytes 1990656 | tf_op jit(solution)/shard_map/all_gather | solution.py:477
  635.7 5.9 copy-start.4
  641.6 17.4 %copy-start.18 = (f32[2,72]{1,0:T(2,128)S(1)}, f32[2,72]{1,0:T(2,128)}, u32[]{:S(2)}) copy-start(f32[2,72]{1,0:T(2,128)} %param.12) | copy-start | bytes 1732
  644.7 34.1 %copy-start.11 = (f32[2,72]{1,0:T(2,128)}, f32[2,72]{1,0:T(2,128)S(1)}, u32[]{:S(2)}) copy-start(f32[2,72]{1,0:T(2,128)S(1)} %get-tuple-element.129) | copy-start | bytes 1732
  678.8 69.4 %copy-start = (f32[72,6144]{1,0:T(8,128)S(1)}, f32[72,6144]{1,0:T(8,128)}, u32[]{:S(2)}) copy-start(f32[72,6144]{1,0:T(8,128)} %param.13) | copy-start | bytes 5308420
  (7 other events, 15.1 us)
Sparse Core Ops, SparseCore 0:
  10.7 44.6 all-gather.7
  57.6 44.4 all-gather.9
  104.9 44.4 all-gather.11
  152.0 44.4 all-gather.13
  255.9 60.0 reduce-scatter.16
  319.8 63.5 reduce-scatter.8
  387.4 65.4 reduce-scatter.10
  457.0 65.4 reduce-scatter.12
  526.5 65.4 reduce-scatter.14
  635.9 42.9 all-gather.15
